TPU v7x, 32 devices: a whole 2x2x4 slice. The times are simulated.
32 devices in a mesh: ctx: 2 (over x), tok: 8 (over z, core), head: 2 (over y).
Axes of the slice: x: 2, y: 2, z: 4, core: 2. Of those that a mesh axis runs over, the one named last changes fastest.
Arguments:
- keys: bfloat16 [2, 2, 4, 6144, 256], P(None, 'ctx', 'head', 'tok'), may hold values from -6 to 6
- values: bfloat16 [2, 2, 4, 6144, 256], P(None, 'ctx', 'head', 'tok'), may hold values from -6 to 6
- queries: bfloat16 [2, 2, 4, 6144, 256], P(None, 'ctx', 'head', 'tok'), may hold values from -6 to 6
- rates: float32 [2, 2, 4, 6144], P(None, 'ctx', 'head', 'tok'), may hold values from 0.1 to 3, as said below
- state_in: bfloat16 [2, 4, 3, 256, 512], P('ctx', 'head'), may hold values from -0.375 to 0.375
- fresh: bfloat16 [4, 3, 256, 512], P('head'), may hold values from -0.375 to 0.375
Outputs:
- outputs: bfloat16 [2, 2, 4, 6144, 256], P(None, 'ctx', 'head', 'tok')
Inputs may be any that keep to these rules, and one draw needn't show every extreme that they name: Positive per-token learning rates.
All inputs are finite; a program needn't handle non-finite values.
Results may differ from a plain program's by a relative error of at most 0.023.
Values may be sent and summed in bfloat16 or wider, within the bound.
No kernel may reach another device: no remote copies, remote signals or barrier semaphores. Data moves between devices by JAX's collectives and lax.ppermute only.
A program may use at most 64 MiB of HBM per device.

v0:
```python
import jax
import jax.numpy as jnp
from jax import lax
from jax.sharding import PartitionSpec as P


def from_behind(value, axis, steps):
    count = lax.axis_size(axis)
    first, last = (max(0, -steps), min(count, count - steps))
    return lax.ppermute(value, axis, [(source, source + steps) for source in range(first, last)])


def partial_grads(state, keys_p, values_p, rate_p):
    h_one = jnp.dot(keys_p, state[0], preferred_element_type=jnp.float32)
    h_three = jnp.dot(keys_p, state[1], preferred_element_type=jnp.float32)
    sig = jax.nn.sigmoid(h_one)
    act = (h_one * sig * h_three).astype(jnp.bfloat16)
    weighted = (rate_p[:, None] * values_p.astype(jnp.float32)).astype(jnp.bfloat16)
    dact = -jnp.dot(weighted, state[2], preferred_element_type=jnp.float32)
    d_one = (dact * h_three * sig * (1.0 + h_one * (1.0 - sig))).astype(jnp.bfloat16)
    d_three = (dact * h_one * sig).astype(jnp.bfloat16)
    contract = (((0,), (0,)), ((), ()))
    g_one = lax.dot_general(keys_p, d_one, contract, preferred_element_type=jnp.float32)
    g_three = lax.dot_general(keys_p, d_three, contract, preferred_element_type=jnp.float32)
    g_back = -lax.dot_general(weighted, act, contract, preferred_element_type=jnp.float32)
    return jnp.stack([g_one, g_three, g_back])


def apply_state(state, queries_h):
    p_one = jnp.dot(queries_h, state[0], preferred_element_type=jnp.float32)
    p_three = jnp.dot(queries_h, state[1], preferred_element_type=jnp.float32)
    mixed = (jax.nn.silu(p_one) * p_three).astype(jnp.bfloat16)
    contract = (((1,), (1,)), ((), ()))
    return lax.dot_general(mixed, state[2], contract, preferred_element_type=jnp.float32).astype(
        jnp.bfloat16
    )


def renormed(older_bf, grads, total_sq, heads_all, hidden):
    scale = 0.5 * jnp.sqrt(jnp.float32(3 * hidden * heads_all)) / jnp.sqrt(total_sq + 1e-06)
    older = older_bf.astype(jnp.float32)
    moved = older - scale * grads
    old_norm = jnp.sqrt(jnp.sum(older * older, axis=-2, keepdims=True))
    new_norm = jnp.sqrt(jnp.sum(moved * moved, axis=-2, keepdims=True) + 1e-06)
    return (moved * old_norm / new_norm).astype(jnp.bfloat16)


def block_tick(state, keys_t, values_t, rates_t, queries_t):
    heads_all = lax.axis_size("head") * state.shape[0]
    hidden = state.shape[3]
    grads = jax.vmap(partial_grads)(state, keys_t, values_t, rates_t)
    summed = lax.psum(grads.astype(jnp.bfloat16), "tok").astype(jnp.float32)
    total_sq = lax.psum(jnp.sum(summed * summed), "head")
    newer = renormed(state, summed, total_sq, heads_all, hidden)
    applied = jax.vmap(apply_state)(newer, queries_t)
    return (newer, applied)


def shards(keys, values, queries, rates, state_in, fresh):
    first_state, first_out = block_tick(
        state_in[0], keys[0, 0], values[0, 0], rates[0, 0], queries[0, 0]
    )
    arrived = from_behind(first_state, "ctx", 1)
    incoming = jnp.where(lax.axis_index("ctx") == 0, fresh, arrived)
    second_state, second_out = block_tick(
        incoming, keys[1, 0], values[1, 0], rates[1, 0], queries[1, 0]
    )
    return jnp.stack([first_out, second_out])[:, None]


def solution(mesh):
    in_specs = (
        P(None, "ctx", "head", "tok", None),
        P(None, "ctx", "head", "tok", None),
        P(None, "ctx", "head", "tok", None),
        P(None, "ctx", "head", "tok"),
        P("ctx", "head", None, None, None),
        P("head", None, None, None),
    )
    out_specs = P(None, "ctx", "head", "tok", None)
    return jax.shard_map(shards, mesh=mesh, in_specs=in_specs, out_specs=out_specs, check_vma=False)
```

profile of v0, /device:TPU:0, one launch (start us, length us, event | category | flops | bytes accessed | tf_op | source)
XLA Modules:
  0.0 232.4 jit_solution(3632334294932788770)
XLA Ops:
  6.5 1.6 copy.54
  11.0 1.4 fusion.63
  12.5 1.6 fusion.52
  14.0 1.2 fusion.56
  15.3 1.3 maximum_bitcast_fusion
  16.6 64.7 %all-reduce.3.cloned.1.call-done = bf16[2,3,256,512]{3,2,0,1:T(8,128)(2,1)} async-done(((bf16[2,3,256,512]{3,2,0,1:T(8,128)(2,1)}), bf16[2,3,256,512]{3,2,0,1:T(8,128)(2,1)}) %all-reduce.3.cloned.1.call-update) | async-done | bytes 1572880 | tf_op jit(solution)/shard_map/psum | solution.py:52
  81.3 2.9 %fusion.1 = f32[]{:T(128)} fusion(bf16[2,3,256,512]{3,2,0,1:T(8,128)(2,1)} %all-reduce.3.cloned.1.call-done), kind=kLoop, calls=%fused_computation.9 | loop fusion | flops 2359295 | bytes 1572868 | tf_op jit(solution)/shard_map/reduce_sum | solution.py:53
  84.2 5.5 %psum.29 = f32[]{:T(128)} all-reduce(f32[]{:T(128)} %fusion.1), channel_id=1, replica_groups=mesh['ctx'=2,'tok'=8,'head'=2] {'head'}, use_global_device_ids=true, to_apply=%region_2.0 | all-reduce | flops 1 | bytes 8 | tf_op jit(solution)/shard_map/psum | solution.py:53
  90.5 2.3 fusion
  92.8 1.8 divide_convert_fusion.1
  94.7 4.6 %collective-permute-start = (bf16[2,3,256,512]{3,2,0,1:T(8,128)(2,1)}, bf16[2,3,256,512]{3,2,0,1:T(8,128)(2,1)}, u32[]{:S(2)}, u32[]{:S(2)}) collective-permute-start(bf16[2,3,256,512]{3,2,0,1:T(8,128)(2,1)} %divide_convert_fusion.1), channel_id=1, source_target_pairs={{0,16},{1,17},{2,18},{3,19},{4,20},{5,21},{6,22},{7,23},{8,24},{9,... | collective-permute-start | bytes 4718600 | tf_op jit(solution)/shard_map/ppermute | solution.py:10
  99.3 30.1 %collective-permute-done = bf16[2,3,256,512]{3,2,0,1:T(8,128)(2,1)} collective-permute-done((bf16[2,3,256,512]{3,2,0,1:T(8,128)(2,1)}, bf16[2,3,256,512]{3,2,0,1:T(8,128)(2,1)}, u32[]{:S(2)}, u32[]{:S(2)}) %collective-permute-start) | collective-permute-done | bytes 1572896 | tf_op jit(solution)/shard_map/ppermute | solution.py:10
  129.4 1.6 copy_select_fusion
  133.6 1.4 fusion.60
  135.1 1.5 fusion.53
  136.6 1.2 fusion.57
  137.8 1.3 maximum_bitcast_fusion.1
  139.8 3.3 %fusion.74 = f32[2,512,768]{1,2,0:T(8,128)} fusion(bf16[2,1,2,768,256]{4,3,2,1,0:T(8,128)(2,1)S(1)} %copy-done.8, bf16[2,3,256,512]{3,2,0,1:T(8,128)(2,1)} %divide_convert_fusion.1), kind=kOutput, calls=%fused_computation.92 | convolution fusion | flops 402653184 | bytes 4456448 | tf_op jit(solution)/shard_map/vmap()/dot_general | solution.py:30
  143.1 59.2 %all-reduce.5.cloned.1.call-done = bf16[2,3,256,512]{3,2,0,1:T(8,128)(2,1)} async-done(((bf16[2,3,256,512]{3,2,0,1:T(8,128)(2,1)}), bf16[2,3,256,512]{3,2,0,1:T(8,128)(2,1)}) %all-reduce.5.cloned.1.call-update) | async-done | bytes 1572880 | tf_op jit(solution)/shard_map/psum | solution.py:52
  202.2 2.8 %fusion.3 = f32[]{:T(128)} fusion(bf16[2,3,256,512]{3,2,0,1:T(8,128)(2,1)} %all-reduce.5.cloned.1.call-done), kind=kLoop, calls=%fused_computation.11 | loop fusion | flops 2359295 | bytes 1572868 | tf_op jit(solution)/shard_map/reduce_sum | solution.py:53
  205.0 4.7 %fusion.46 = bf16[1,2,768,256]{3,2,1,0:T(8,128)(2,1)} fusion(f32[2,512,768]{1,2,0:T(8,128)} %fusion.74, bf16[2,1,2,768,256]{4,3,2,1,0:T(8,128)(2,1)} %param.8, bf16[2,3,256,512]{3,2,0,1:T(8,128)(2,1)} %divide_convert_fusion.1), kind=kOutput, calls=%fused_computation.73 | convolution fusion | flops 810418176 | bytes 5767168 | tf_op jit(solution)/shard_map/vmap()/dot_general | solution.py:34
  209.7 5.5 %psum.31 = f32[]{:T(128)} all-reduce(f32[]{:T(128)} %fusion.3), channel_id=1, replica_groups=mesh['ctx'=2,'tok'=8,'head'=2] {'head'}, use_global_device_ids=true, to_apply=%region_7.8 | all-reduce | flops 1 | bytes 8 | tf_op jit(solution)/shard_map/psum | solution.py:53
  219.3 3.6 %fusion.47 = bf16[1,2,768,256]{3,2,1,0:T(8,128)(2,1)} fusion(f32[2,512,768]{1,2,0:T(8,128)S(1)} %fusion.64, bf16[2,1,2,768,256]{4,3,2,1,0:T(8,128)(2,1)} %param.8, bf16[2,3,256,512]{3,2,0,1:T(8,128)(2,1)} %copy-done.5), kind=kOutput, calls=%fused_computation.74 | convolution fusion | flops 810418176 | bytes 5767168 | tf_op jit(solution)/shard_map/vmap()/dot_general | solution.py:34
  222.9 2.7 %maximum_bitcast_fusion.2 = bf16[2,1,2,768,256]{4,3,2,1,0:T(8,128)(2,1)} fusion(bf16[1,2,768,256]{3,2,1,0:T(8,128)(2,1)} %fusion.47, bf16[1,2,768,256]{3,2,1,0:T(8,128)(2,1)} %fusion.46), kind=kLoop, calls=%fused_computation.52 | loop fusion | flops 786432 | bytes 3145728 | tf_op jit(solution)/shard_map/broadcast_in_dim | solution.py:68
  (40 shorter events, 9.5 us)
Async XLA Ops:
  6.5 1.9 copy-start.3
  6.5 74.8 %all-reduce.3.cloned.1.call-start = ((), (), s32[]{:S(2)}) async-start(), calls=%async_computation | async-start | bytes 3145728 | tf_op jit(solution)/shard_map/psum | solution.py:52
  9.0 0.7 copy-start.10
  9.0 1.4 copy-start.6
  15.2 75.2 %copy-start = (bf16[1,2,3,256,512]{4,3,2,1,0:T(8,128)(2,1)S(1)}, bf16[1,2,3,256,512]{4,3,2,1,0:T(8,128)(2,1)}, u32[]{:S(2)}) copy-start(bf16[1,2,3,256,512]{4,3,2,1,0:T(8,128)(2,1)} %param.10) | copy-start | bytes 4718596
  16.6 185.7 %all-reduce.5.cloned.1.call-start = ((), (), s32[]{:S(2)}) async-start(), calls=%async_computation.1 | async-start | bytes 3145728 | tf_op jit(solution)/shard_map/psum | solution.py:52
  81.3 11.5 %copy-start.2 = (bf16[2,3,256,512]{3,2,0,1:T(8,128)(2,1)S(1)}, bf16[2,3,256,512]{3,2,0,1:T(8,128)(2,1)}, u32[]{:S(2)}) copy-start(bf16[2,3,256,512]{3,2,0,1:T(8,128)(2,1)} %all-reduce.3.cloned.1.call-done) | copy-start | bytes 4718596
  94.7 36.4 %copy-start.4 = (bf16[2,1,2,768,256]{4,3,2,1,0:T(8,128)(2,1)S(1)}, bf16[2,1,2,768,256]{4,3,2,1,0:T(8,128)(2,1)}, u32[]{:S(2)}) copy-start(bf16[2,1,2,768,256]{4,3,2,1,0:T(8,128)(2,1)} %param.6) | copy-start | bytes 4718596
  94.7 34.8 %collective-permute-start = (bf16[2,3,256,512]{3,2,0,1:T(8,128)(2,1)}, bf16[2,3,256,512]{3,2,0,1:T(8,128)(2,1)}, u32[]{:S(2)}, u32[]{:S(2)}) collective-permute-start(bf16[2,3,256,512]{3,2,0,1:T(8,128)(2,1)} %divide_convert_fusion.1), channel_id=1, source_target_pairs={{0,16},{1,17},{2,18},{3,19},{4,20},{5,21},{6,22},{7,23},{8,24},{9,... | collective-permute-start | bytes 4718600 | tf_op jit(solution)/shard_map/ppermute | solution.py:10
  131.6 1.4 copy-start.7
  137.8 2.0 copy-start.8
  205.0 10.9 %copy-start.1 = (bf16[2,3,256,512]{3,2,0,1:T(8,128)(2,1)S(1)}, bf16[2,3,256,512]{3,2,0,1:T(8,128)(2,1)}, u32[]{:S(2)}) copy-start(bf16[2,3,256,512]{3,2,0,1:T(8,128)(2,1)} %all-reduce.5.cloned.1.call-done) | copy-start | bytes 4718596
  216.9 1.9 copy-start.9
  217.6 1.1 copy-start.5
Sparse Core Ops, SparseCore 0:
  16.7 64.5 all-reduce.2
  139.3 62.8 all-reduce.4
where the time goes:
time: 233 us; the launch traced here: 232 us
  waiting for transfers between devices  154 us (66%)
  matrix products  24.1 us (10%)
  other arithmetic  18.3 us (8%)
  between operations  15 us (6%)
  blocking collectives  11.1 us (5%)
  local copies, waits for them, and re-layouts  5.34 us (2%)
  starting transfers between devices  4.68 us (2%)
    psum x2, waiting for transfers between devices, block_tick(): summed = lax.psum(grads.astype(jnp.bfloat16), 'tok').astype(jnp.float32)  124 us
    ppermute x1, waiting for transfers between devices, from_behind(): lax.ppermute(value, axis, [(source, source + steps) for source in range(f...  30.1 us
    psum x2, blocking collectives, block_tick(): total_sq = lax.psum(jnp.sum(summed * summed), 'head')  11.1 us
    dot_general x2, matrix products, apply_state(): lax.dot_general(mixed, state[2], contract, preferred_element_type=jnp.flo...  8.33 us
    reduce_sum x2, other arithmetic, block_tick(): total_sq = lax.psum(jnp.sum(summed * summed), 'head')  5.73 us
    unnamed x23, local copies, waits for them, and re-layouts  5.3 us
  transfers between devices with their start and end apart: 3, of which 3 were waited for; matrix products, arithmetic and copies ran while one was open for 1% of the time, Pallas kernels for 0%

commit v1 on v0

--- a/solution.py
+++ b/solution.py
@@ -49,7 +49,11 @@
     heads_all = lax.axis_size("head") * state.shape[0]
     hidden = state.shape[3]
     grads = jax.vmap(partial_grads)(state, keys_t, values_t, rates_t)
-    summed = lax.psum(grads.astype(jnp.bfloat16), "tok").astype(jnp.float32)
+    summed = (
+        jax.lax.all_gather(grads.astype(jnp.bfloat16), axis_name="tok")
+        .sum(axis=0)
+        .astype(jnp.float32)
+    )
     total_sq = lax.psum(jnp.sum(summed * summed), "head")
     newer = renormed(state, summed, total_sq, heads_all, hidden)
     applied = jax.vmap(apply_state)(newer, queries_t)

time: 233 us -> 359 us (1.54)
  waiting for transfers between devices: 154 us -> 264 us
  other arithmetic: 18.3 us -> 30.2 us
    all_gather x0 -> x2, waiting for transfers between devices: none -> 232 us  [block_tick(): jax.lax.all_gather(grads.astype(jnp.bfloat16), axis_name='tok').sum(axis=0)]
    psum x2 -> x0, waiting for transfers between devices: 124 us -> none  [block_tick(): summed = lax.psum(grads.astype(jnp.bfloat16), 'tok').astype(jnp.float32)]
    reduce_sum x0 -> x2, other arithmetic: none -> 16.1 us  [block_tick(): summed = jax.lax.all_gather(grads.astype(jnp.bfloat16), axis_name='tok')....]
where the time goes in v1:
time: 359 us; the launch traced here: 358 us
  waiting for transfers between devices  264 us (74%)
  other arithmetic  30.2 us (8%)
  matrix products  24.2 us (7%)
  between operations  15 us (4%)
  blocking collectives  11.3 us (3%)
  local copies, waits for them, and re-layouts  8.92 us (2%)
  starting transfers between devices  4.7 us (1%)
    all_gather x2, waiting for transfers between devices, block_tick(): jax.lax.all_gather(grads.astype(jnp.bfloat16), axis_name='tok').sum(axis=0)  232 us
    ppermute x1, waiting for transfers between devices, from_behind(): lax.ppermute(value, axis, [(source, source + steps) for source in range(f...  32.1 us
    reduce_sum x2, other arithmetic, block_tick(): summed = jax.lax.all_gather(grads.astype(jnp.bfloat16), axis_name='tok')....  16.1 us
    psum x2, blocking collectives, block_tick(): total_sq = lax.psum(jnp.sum(summed * summed), 'head')  11.3 us
    dot_general x2, matrix products, apply_state(): lax.dot_general(mixed, state[2], contract, preferred_element_type=jnp.flo...  8.23 us
  transfers between devices with their start and end apart: 3, of which 3 were waited for; matrix products, arithmetic and copies ran while one was open for 1% of the time, Pallas kernels for 0%

profile of v1, /device:TPU:0, one launch (start us, length us, event | category | flops | bytes accessed | tf_op | source)
XLA Modules:
  0.0 358.5 jit_solution(18054076712388055410)
XLA Ops:
  6.5 1.6 copy.71
  11.0 1.3 fusion.63
  12.4 1.7 fusion.52
  16.7 119.5 %all-gather.5.cloned.1.call-done = bf16[16,3,256,512]{2,3,0,1:T(8,128)(2,1)} async-done(((bf16[2,3,256,512]{2,3,0,1:T(8,128)(2,1)}), bf16[16,3,256,512]{2,3,0,1:T(8,128)(2,1)}) %all-gather.5.cloned.1.call-update) | async-done | bytes 12582928 | tf_op jit(solution)/shard_map/all_gather | solution.py:53
  136.3 8.1 %reduce_sum.78 = bf16[2,3,256,512]{2,3,0,1:T(8,128)(2,1)} reduce(bf16[8,2,3,256,512]{3,4,1,0,2:T(8,128)(2,1)} %bitcast.234, bf16[]{:T(256)} %constant.7.clone.1), dimensions={0}, to_apply=%region_0.0 | reduce | flops 5505024 | bytes 14155778 | tf_op jit(solution)/shard_map/reduce_sum | solution.py:54
  144.3 1.8 copy.31
  146.2 1.4 fusion.1
  147.6 5.5 %psum.14 = f32[]{:T(128)} all-reduce(f32[]{:T(128)} %fusion.1), channel_id=1, replica_groups=mesh['ctx'=2,'tok'=8,'head'=2] {'head'}, use_global_device_ids=true, to_apply=%region_2.0 | all-reduce | flops 1 | bytes 8 | tf_op jit(solution)/shard_map/psum | solution.py:57
  154.7 1.8 divide_convert_fusion.1
  156.6 4.7 %collective-permute-start = (bf16[2,3,256,512]{3,2,0,1:T(8,128)(2,1)}, bf16[2,3,256,512]{3,2,0,1:T(8,128)(2,1)}, u32[]{:S(2)}, u32[]{:S(2)}) collective-permute-start(bf16[2,3,256,512]{3,2,0,1:T(8,128)(2,1)} %divide_convert_fusion.1), channel_id=1, source_target_pairs={{0,16},{1,17},{2,18},{3,19},{4,20},{5,21},{6,22},{7,23},{8,24},{9,... | collective-permute-start | bytes 4718600 | tf_op jit(solution)/shard_map/ppermute | solution.py:10
  161.2 32.1 %collective-permute-done = bf16[2,3,256,512]{3,2,0,1:T(8,128)(2,1)} collective-permute-done((bf16[2,3,256,512]{3,2,0,1:T(8,128)(2,1)}, bf16[2,3,256,512]{3,2,0,1:T(8,128)(2,1)}, u32[]{:S(2)}, u32[]{:S(2)}) %collective-permute-start) | collective-permute-done | bytes 1572896 | tf_op jit(solution)/shard_map/ppermute | solution.py:10
  193.3 1.6 copy_select_fusion
  197.5 1.3 fusion.60
  198.8 1.7 fusion.53
  201.8 1.3 maximum_bitcast_fusion.1
  203.8 3.3 fusion.74
  207.0 112.6 %all-gather.7.cloned.1.call-done = bf16[16,3,256,512]{2,3,0,1:T(8,128)(2,1)} async-done(((bf16[2,3,256,512]{2,3,0,1:T(8,128)(2,1)}), bf16[16,3,256,512]{2,3,0,1:T(8,128)(2,1)}) %all-gather.7.cloned.1.call-update) | async-done | bytes 12582928 | tf_op jit(solution)/shard_map/all_gather | solution.py:53
  319.7 8.1 %reduce_sum.82 = bf16[2,3,256,512]{2,3,0,1:T(8,128)(2,1)} reduce(bf16[8,2,3,256,512]{3,4,1,0,2:T(8,128)(2,1)} %bitcast.235, bf16[]{:T(256)} %constant.7.clone.1), dimensions={0}, to_apply=%region_5.6 | reduce | flops 5505024 | bytes 14155778 | tf_op jit(solution)/shard_map/reduce_sum | solution.py:54
  327.7 1.7 copy.43
  329.5 1.5 fusion.3
  330.9 4.6 %fusion.46 = bf16[1,2,768,256]{3,2,1,0:T(8,128)(2,1)} fusion(f32[2,512,768]{1,2,0:T(8,128)} %fusion.74, bf16[2,1,2,768,256]{4,3,2,1,0:T(8,128)(2,1)} %param.8, bf16[2,3,256,512]{3,2,0,1:T(8,128)(2,1)} %divide_convert_fusion.1), kind=kOutput, calls=%fused_computation.73 | convolution fusion | flops 810418176 | bytes 5767168 | tf_op jit(solution)/shard_map/vmap()/dot_general | solution.py:34
  335.5 5.8 %psum.15 = f32[]{:T(128)} all-reduce(f32[]{:T(128)} %fusion.3), channel_id=1, replica_groups=mesh['ctx'=2,'tok'=8,'head'=2] {'head'}, use_global_device_ids=true, to_apply=%region_7.8 | all-reduce | flops 1 | bytes 8 | tf_op jit(solution)/shard_map/psum | solution.py:57
  345.3 3.7 %fusion.47 = bf16[1,2,768,256]{3,2,1,0:T(8,128)(2,1)} fusion(f32[2,512,768]{1,2,0:T(8,128)S(1)} %fusion.64, bf16[2,1,2,768,256]{4,3,2,1,0:T(8,128)(2,1)} %param.8, bf16[2,3,256,512]{3,2,0,1:T(8,128)(2,1)} %copy-done.3), kind=kOutput, calls=%fused_computation.74 | convolution fusion | flops 810418176 | bytes 5767168 | tf_op jit(solution)/shard_map/vmap()/dot_general | solution.py:34
  349.0 2.7 maximum_bitcast_fusion.2
  (40 shorter events, 14.2 us)
Async XLA Ops:
  6.5 1.9 copy-start.1
  6.5 129.7 %all-gather.5.cloned.1.call-start = ((), (), s32[]{:S(2)}) async-start(), calls=%async_computation | async-start | bytes 14155776 | tf_op jit(solution)/shard_map/all_gather | solution.py:53
  9.0 0.7 copy-start.8
  9.0 1.4 copy-start.4
  16.7 303.0 %all-gather.7.cloned.1.call-start = ((), (), s32[]{:S(2)}) async-start(), calls=%async_computation.1 | async-start | bytes 14155776 | tf_op jit(solution)/shard_map/all_gather | solution.py:53
  144.3 9.5 %copy-start = (bf16[1,2,3,256,512]{4,3,2,1,0:T(8,128)(2,1)S(1)}, bf16[1,2,3,256,512]{4,3,2,1,0:T(8,128)(2,1)}, u32[]{:S(2)}) copy-start(bf16[1,2,3,256,512]{4,3,2,1,0:T(8,128)(2,1)} %param.10) | copy-start | bytes 4718596
  156.6 38.3 %copy-start.2 = (bf16[2,1,2,768,256]{4,3,2,1,0:T(8,128)(2,1)S(1)}, bf16[2,1,2,768,256]{4,3,2,1,0:T(8,128)(2,1)}, u32[]{:S(2)}) copy-start(bf16[2,1,2,768,256]{4,3,2,1,0:T(8,128)(2,1)} %param.6) | copy-start | bytes 4718596
  156.6 36.7 %collective-permute-start = (bf16[2,3,256,512]{3,2,0,1:T(8,128)(2,1)}, bf16[2,3,256,512]{3,2,0,1:T(8,128)(2,1)}, u32[]{:S(2)}, u32[]{:S(2)}) collective-permute-start(bf16[2,3,256,512]{3,2,0,1:T(8,128)(2,1)} %divide_convert_fusion.1), channel_id=1, source_target_pairs={{0,16},{1,17},{2,18},{3,19},{4,20},{5,21},{6,22},{7,23},{8,24},{9,... | collective-permute-start | bytes 4718600 | tf_op jit(solution)/shard_map/ppermute | solution.py:10
  195.4 1.4 copy-start.5
  201.8 2.0 copy-start.6
  342.9 1.9 copy-start.7
  343.6 1.1 copy-start.3
Sparse Core Ops, SparseCore 0:
  16.8 119.4 all-gather.4
  203.3 116.3 all-gather.6
